TPU v7x, 32 devices: a whole 2x2x4 slice. The times are simulated.
32 devices in a mesh: dp: 4 (over y, core), row: 2 (over x), col: 4 (over z).
Axes of the slice: x: 2, y: 2, z: 4, core: 2. Of those that a mesh axis runs over, the one named last changes fastest.
Arguments:
- tokens: float32 [16384, 1024], P(('dp', 'row', 'col')), may hold values from -6 to 6
- segment_ids: int32 [16384], P(('dp', 'row', 'col')), may hold values from 0 to 127, never falling along the last dimension, each value on 1 to 512 neighbouring positions
- cotangent: float32 [16384, 1024], P(('dp', 'row', 'col')), may hold values from -6 to 6
- weight_query: float32 [1024, 1024], P('row', 'col'), as said below
- weight_key: float32 [1024, 1024], P('row', 'col'), may hold values from -0.1875 to 0.1875
- weight_value: float32 [1024, 1024], P('row', 'col'), may hold values from -0.1875 to 0.1875
- weight_output: float32 [1024, 1024], P('row', 'col'), may hold values from -0.75 to 0.75
- weight_inner: float32 [1024, 4096], P('row', 'col'), may hold values from -0.1875 to 0.1875
- weight_outer: float32 [4096, 1024], P('row', 'col'), may hold values from -0.09375 to 0.09375
- bias_query: float32 [1024], P(('row', 'col')), may hold values from -1.5 to 1.5
- bias_value: float32 [1024], P(('row', 'col')), may hold values from -1.5 to 1.5
- bias_output: float32 [1024], P(('row', 'col')), may hold values from -1.5 to 1.5
- bias_inner: float32 [4096], P(('row', 'col')), may hold values from -1.5 to 1.5
- bias_outer: float32 [1024], P(('row', 'col')), may hold values from -1.5 to 1.5
- gain_attn: float32 [1024], P(('row', 'col')), may hold values from 0.25 to 1.75
- shift_attn: float32 [1024], P(('row', 'col')), may hold values from -1.5 to 1.5
- gain_block: float32 [1024], P(('row', 'col')), may hold values from 0.25 to 1.75
- shift_block: float32 [1024], P(('row', 'col')), may hold values from -1.5 to 1.5
- tau_num: int32 [1], replicated, may hold values from 100 to 399
- tau_den: int32 [1], replicated, may hold values from 400 to 999
Outputs:
- output: float32 [16384, 1024], P(('dp', 'row', 'col'))
- grad_tokens: float32 [16384, 1024], P(('dp', 'row', 'col'))
- grad_weight_query: float32 [1024, 1024], P('row', 'col')
- grad_weight_key: float32 [1024, 1024], P('row', 'col')
- grad_weight_value: float32 [1024, 1024], P('row', 'col')
- grad_weight_output: float32 [1024, 1024], P('row', 'col')
- grad_weight_inner: float32 [1024, 4096], P('row', 'col')
- grad_weight_outer: float32 [4096, 1024], P('row', 'col')
- grad_bias_query: float32 [1024], P(('row', 'col'))
- grad_bias_value: float32 [1024], P(('row', 'col'))
- grad_bias_output: float32 [1024], P(('row', 'col'))
- grad_bias_inner: float32 [4096], P(('row', 'col'))
- grad_bias_outer: float32 [1024], P(('row', 'col'))
- grad_gain_attn: float32 [1024], P(('row', 'col'))
- grad_shift_attn: float32 [1024], P(('row', 'col'))
- grad_gain_block: float32 [1024], P(('row', 'col'))
- grad_shift_block: float32 [1024], P(('row', 'col'))
- head_peak: float32 [16], replicated
- clipped_query: float32 [1024, 1024], P('row', 'col')
- clipped_key: float32 [1024, 1024], P('row', 'col')
Inputs may be any that keep to these rules, and one draw needn't show every extreme that they name: `segment_ids`: along the tokens the numbers never fall; each document covers 1 to 512 consecutive tokens, one exactly 512. `weight_query`: entries within 18 / sqrt(1024) in magnitude.
All inputs are finite; a program needn't handle non-finite values.
Results may differ from a plain program's by a relative error of at most 0.019.
The roundings to bfloat16 on the way count: a program that leaves them out, or rounds other values in their place, can miss the bound.
Values may be sent and summed in bfloat16 or wider, within the bound.
A program may use at most 256 MiB of HBM per device.

v0:
```python
import jax
import jax.numpy as jnp
from jax import lax
from jax.sharding import PartitionSpec as P

H = 16
DH = 64
SEQ = 512
norm_eps = 1e-12
neg_fill = -1e30


def norm_rows(values, gain_vec, shift_vec):
    center = values - jnp.mean(values, axis=-1, keepdims=True)
    spread = jnp.mean(center * center, axis=-1, keepdims=True)
    return center * lax.rsqrt(spread + norm_eps) * gain_vec + shift_vec


def gelu_exact(values):
    return jax.nn.gelu(values, approximate=False)


def apply_weight(operand, weight):
    row_count, col_count, rows_in, cols_out = weight.shape
    token_count = operand.shape[0]
    result = jnp.einsum(
        "trk,rckn->tcn",
        operand.reshape(token_count, row_count, rows_in),
        weight,
        preferred_element_type=jnp.float32,
    )
    return result.reshape(token_count, col_count * cols_out)


def apply_back(gradient, weight):
    row_count, col_count, rows_in, cols_out = weight.shape
    token_count = gradient.shape[0]
    result = jnp.einsum(
        "tcn,rckn->trk",
        gradient.reshape(token_count, col_count, cols_out),
        weight,
        preferred_element_type=jnp.float32,
    )
    return result.reshape(token_count, row_count * rows_in)


def weight_term(operand, gradient, row_count, col_count, pieces):
    token_count, width_in = operand.shape
    width_out = gradient.shape[1]
    piece_rows = width_in // (row_count * pieces)
    left_blocks = operand.reshape(token_count, row_count, pieces, piece_rows)
    right_blocks = gradient.reshape(token_count, col_count, width_out // col_count)
    term = jnp.einsum(
        "trdk,tcn->drckn", left_blocks, right_blocks, preferred_element_type=jnp.float32
    )
    return term.reshape(pieces * row_count * col_count, piece_rows, width_out // col_count)


def vector_term(vector, group_count, pieces):
    return (
        vector.reshape(group_count, pieces, -1).transpose(1, 0, 2).reshape(pieces * group_count, -1)
    )


def column_sum(gradient_low):
    return jnp.sum(gradient_low, axis=0, dtype=jnp.float32)


def to_wire(block):
    return block.astype(jnp.bfloat16)[None]


def unpack(gathered, row_count, col_count):
    matrices = tuple(
        (
            shard_item.reshape(row_count, col_count, shard_item.shape[1], shard_item.shape[2])
            for shard_item in gathered[:6]
        )
    )
    vectors = tuple((shard_item.reshape(-1).astype(jnp.float32) for shard_item in gathered[6:]))
    return matrices + vectors


def fetch_params(wire_items):
    return (
        lax.all_gather(wire_items[0], ("row", "col"), axis=0, tiled=True),
        lax.all_gather(wire_items[1], ("row", "col"), axis=0, tiled=True),
        lax.all_gather(wire_items[2], ("row", "col"), axis=0, tiled=True),
        lax.all_gather(wire_items[3], ("row", "col"), axis=0, tiled=True),
        lax.all_gather(wire_items[4], ("row", "col"), axis=0, tiled=True),
        lax.all_gather(wire_items[5], ("row", "col"), axis=0, tiled=True),
        lax.all_gather(wire_items[6], ("row", "col"), axis=0, tiled=True),
        lax.all_gather(wire_items[7], ("row", "col"), axis=0, tiled=True),
        lax.all_gather(wire_items[8], ("row", "col"), axis=0, tiled=True),
        lax.all_gather(wire_items[9], ("row", "col"), axis=0, tiled=True),
        lax.all_gather(wire_items[10], ("row", "col"), axis=0, tiled=True),
        lax.all_gather(wire_items[11], ("row", "col"), axis=0, tiled=True),
        lax.all_gather(wire_items[12], ("row", "col"), axis=0, tiled=True),
        lax.all_gather(wire_items[13], ("row", "col"), axis=0, tiled=True),
        lax.all_gather(wire_items[14], ("row", "col"), axis=0, tiled=True),
    )


def masked_scores(query_heads, key_heads, allowed):
    scores = jnp.einsum(
        "sqhd,skhd->shqk", query_heads, key_heads, preferred_element_type=jnp.float32
    ) * DH ** (-0.5)
    return jnp.where(allowed, scores, neg_fill)


def on_device(
    tokens,
    segment_ids,
    cotangent,
    weight_query,
    weight_key,
    weight_value,
    weight_output,
    weight_inner,
    weight_outer,
    bias_query,
    bias_value,
    bias_output,
    bias_inner,
    bias_outer,
    gain_attn,
    shift_attn,
    gain_block,
    shift_block,
    tau_num,
    tau_den,
):
    row_count = lax.axis_size("row")
    col_count = lax.axis_size("col")
    group_count = row_count * col_count
    wire_items = tuple(
        (
            to_wire(block)
            for block in (
                weight_query,
                weight_key,
                weight_value,
                weight_output,
                weight_inner,
                weight_outer,
                bias_query,
                bias_value,
                bias_output,
                bias_inner,
                bias_outer,
                gain_attn,
                shift_attn,
                gain_block,
                shift_block,
            )
        )
    )
    params_full = unpack(fetch_params(wire_items), row_count, col_count)
    (
        whole_query,
        whole_key,
        whole_value,
        whole_output,
        whole_inner,
        whole_outer,
        add_query,
        add_value,
        add_output,
        add_inner,
        add_outer,
        scale_attn,
        offset_attn,
        scale_block,
        offset_block,
    ) = params_full
    token_count = tokens.shape[0]
    seq_count = token_count // SEQ
    head_shape = (seq_count, SEQ, H, DH)
    token_low = tokens.astype(jnp.bfloat16)
    query_low = (apply_weight(token_low, whole_query) + add_query).astype(jnp.bfloat16)
    key_low = apply_weight(token_low, whole_key).astype(jnp.bfloat16)
    value_low = (apply_weight(token_low, whole_value) + add_value).astype(jnp.bfloat16)
    query_heads = query_low.reshape(head_shape)
    key_heads = key_low.reshape(head_shape)
    value_heads = value_low.reshape(head_shape)
    segment_rows = segment_ids.reshape(seq_count, SEQ)
    allowed = (segment_rows[:, :, None] == segment_rows[:, None, :])[:, None, :, :]
    masked = masked_scores(query_heads, key_heads, allowed)
    local_top = jnp.max(masked, axis=(0, 2, 3))
    row_top = jnp.max(masked, axis=-1, keepdims=True)
    raised = jnp.exp(masked - row_top)
    row_total = jnp.sum(raised, axis=-1, keepdims=True)
    attend = raised / row_total
    log_total = row_top + jnp.log(row_total)
    context = jnp.einsum(
        "shqk,skhd->sqhd",
        attend.astype(jnp.bfloat16),
        value_heads,
        preferred_element_type=jnp.float32,
    )
    context_low = context.reshape(token_count, H * DH).astype(jnp.bfloat16)
    first_sum = tokens + apply_weight(context_low, whole_output) + add_output
    normed = norm_rows(first_sum, scale_attn, offset_attn)
    normed_low = normed.astype(jnp.bfloat16)
    hidden_pre = apply_weight(normed_low, whole_inner) + add_inner
    activated_low = gelu_exact(hidden_pre).astype(jnp.bfloat16)
    second_sum = normed + apply_weight(activated_low, whole_outer) + add_outer
    output = norm_rows(second_sum, scale_block, offset_block)
    head_peak = lax.pmax(local_top, ("dp", "row", "col"))
    back_query, back_key, back_value, back_output, back_inner, back_outer = params_full[:6]
    grad_second, grad_scale_block, grad_offset_block = jax.vjp(
        norm_rows, second_sum, scale_block, offset_block
    )[1](cotangent)
    outer_grad_low = grad_second.astype(jnp.bfloat16)
    act_grad = apply_back(outer_grad_low, back_outer)
    hidden_grad_low = jax.vjp(gelu_exact, hidden_pre)[1](act_grad)[0].astype(jnp.bfloat16)
    normed_grad = grad_second + apply_back(hidden_grad_low, back_inner)
    grad_first, grad_scale_attn, grad_offset_attn = jax.vjp(
        norm_rows, first_sum, scale_attn, offset_attn
    )[1](normed_grad)
    branch_grad_low = grad_first.astype(jnp.bfloat16)
    context_grad_low = apply_back(branch_grad_low, back_output).astype(jnp.bfloat16)
    masked_again = masked_scores(query_heads, key_heads, allowed)
    attend_again = jnp.exp(masked_again - log_total)
    attend_low = attend_again.astype(jnp.bfloat16)
    context_grad_heads = context_grad_low.reshape(head_shape)
    value_grad = jnp.einsum(
        "shqk,sqhd->skhd", attend_low, context_grad_heads, preferred_element_type=jnp.float32
    )
    attend_grad = jnp.einsum(
        "sqhd,skhd->shqk", context_grad_heads, value_heads, preferred_element_type=jnp.float32
    )
    score_grad = attend_again * (
        attend_grad - jnp.sum(attend_again * attend_grad, axis=-1, keepdims=True)
    )
    score_grad_low = score_grad.astype(jnp.bfloat16)
    query_grad = jnp.einsum(
        "shqk,skhd->sqhd", score_grad_low, key_heads, preferred_element_type=jnp.float32
    ) * DH ** (-0.5)
    key_grad = jnp.einsum(
        "shqk,sqhd->skhd", score_grad_low, query_heads, preferred_element_type=jnp.float32
    ) * DH ** (-0.5)
    query_grad_low = query_grad.reshape(token_count, H * DH).astype(jnp.bfloat16)
    key_grad_low = key_grad.reshape(token_count, H * DH).astype(jnp.bfloat16)
    value_grad_low = value_grad.reshape(token_count, H * DH).astype(jnp.bfloat16)
    grad_tokens = (
        grad_first
        + apply_back(query_grad_low, back_query)
        + apply_back(key_grad_low, back_key)
        + apply_back(value_grad_low, back_value)
    )
    pieces = 1
    terms = (
        weight_term(token_low, query_grad_low, row_count, col_count, pieces),
        weight_term(token_low, key_grad_low, row_count, col_count, pieces),
        weight_term(token_low, value_grad_low, row_count, col_count, pieces),
        weight_term(context_low, branch_grad_low, row_count, col_count, pieces),
        weight_term(normed_low, hidden_grad_low, row_count, col_count, pieces),
        weight_term(activated_low, outer_grad_low, row_count, col_count, pieces),
        vector_term(column_sum(query_grad_low), group_count, pieces),
        vector_term(column_sum(value_grad_low), group_count, pieces),
        vector_term(column_sum(branch_grad_low), group_count, pieces),
        vector_term(column_sum(hidden_grad_low), group_count, pieces),
        vector_term(column_sum(outer_grad_low), group_count, pieces),
        vector_term(grad_scale_attn, group_count, pieces),
        vector_term(grad_offset_attn, group_count, pieces),
        vector_term(grad_scale_block, group_count, pieces),
        vector_term(grad_offset_block, group_count, pieces),
    )
    parted = (
        lax.psum_scatter(
            terms[0].astype(jnp.bfloat16), ("row", "col"), scatter_dimension=0, tiled=True
        ).astype(jnp.float32),
        lax.psum_scatter(
            terms[1].astype(jnp.bfloat16), ("row", "col"), scatter_dimension=0, tiled=True
        ).astype(jnp.float32),
        lax.psum_scatter(
            terms[2].astype(jnp.bfloat16), ("row", "col"), scatter_dimension=0, tiled=True
        ).astype(jnp.float32),
        lax.psum_scatter(
            terms[3].astype(jnp.bfloat16), ("row", "col"), scatter_dimension=0, tiled=True
        ).astype(jnp.float32),
        lax.psum_scatter(
            terms[4].astype(jnp.bfloat16), ("row", "col"), scatter_dimension=0, tiled=True
        ).astype(jnp.float32),
        lax.psum_scatter(
            terms[5].astype(jnp.bfloat16), ("row", "col"), scatter_dimension=0, tiled=True
        ).astype(jnp.float32),
        lax.psum_scatter(
            terms[6].astype(jnp.bfloat16), ("row", "col"), scatter_dimension=0, tiled=True
        ).astype(jnp.float32),
        lax.psum_scatter(
            terms[7].astype(jnp.bfloat16), ("row", "col"), scatter_dimension=0, tiled=True
        ).astype(jnp.float32),
        lax.psum_scatter(
            terms[8].astype(jnp.bfloat16), ("row", "col"), scatter_dimension=0, tiled=True
        ).astype(jnp.float32),
        lax.psum_scatter(
            terms[9].astype(jnp.bfloat16), ("row", "col"), scatter_dimension=0, tiled=True
        ).astype(jnp.float32),
        lax.psum_scatter(
            terms[10].astype(jnp.bfloat16), ("row", "col"), scatter_dimension=0, tiled=True
        ).astype(jnp.float32),
        lax.psum_scatter(
            terms[11].astype(jnp.bfloat16), ("row", "col"), scatter_dimension=0, tiled=True
        ).astype(jnp.float32),
        lax.psum_scatter(
            terms[12].astype(jnp.bfloat16), ("row", "col"), scatter_dimension=0, tiled=True
        ).astype(jnp.float32),
        lax.psum_scatter(
            terms[13].astype(jnp.bfloat16), ("row", "col"), scatter_dimension=0, tiled=True
        ).astype(jnp.float32),
        lax.psum_scatter(
            terms[14].astype(jnp.bfloat16), ("row", "col"), scatter_dimension=0, tiled=True
        ).astype(jnp.float32),
    )
    summed = (
        lax.psum(parted[0][0].astype(jnp.bfloat16), "dp").astype(jnp.float32),
        lax.psum(parted[1][0].astype(jnp.bfloat16), "dp").astype(jnp.float32),
        lax.psum(parted[2][0].astype(jnp.bfloat16), "dp").astype(jnp.float32),
        lax.psum(parted[3][0].astype(jnp.bfloat16), "dp").astype(jnp.float32),
        lax.psum(parted[4][0].astype(jnp.bfloat16), "dp").astype(jnp.float32),
        lax.psum(parted[5][0].astype(jnp.bfloat16), "dp").astype(jnp.float32),
        lax.psum(parted[6][0].astype(jnp.bfloat16), "dp").astype(jnp.float32),
        lax.psum(parted[7][0].astype(jnp.bfloat16), "dp").astype(jnp.float32),
        lax.psum(parted[8][0].astype(jnp.bfloat16), "dp").astype(jnp.float32),
        lax.psum(parted[9][0].astype(jnp.bfloat16), "dp").astype(jnp.float32),
        lax.psum(parted[10][0].astype(jnp.bfloat16), "dp").astype(jnp.float32),
        lax.psum(parted[11][0].astype(jnp.bfloat16), "dp").astype(jnp.float32),
        lax.psum(parted[12][0].astype(jnp.bfloat16), "dp").astype(jnp.float32),
        lax.psum(parted[13][0].astype(jnp.bfloat16), "dp").astype(jnp.float32),
        lax.psum(parted[14][0].astype(jnp.bfloat16), "dp").astype(jnp.float32),
    )
    tau_value = tau_num[0].astype(jnp.float32) / tau_den[0].astype(jnp.float32)
    factor = jnp.sqrt(tau_value / jnp.maximum(head_peak, tau_value))
    col_width = weight_query.shape[1]
    col_heads = (lax.axis_index("col") * col_width + jnp.arange(col_width, dtype=jnp.int32)) // DH
    column_factor = jnp.sum(
        jnp.where(
            col_heads[:, None] == jnp.arange(H, dtype=jnp.int32)[None, :], factor[None, :], 0.0
        ),
        axis=1,
    )
    return (
        output,
        grad_tokens,
        summed[0],
        summed[1],
        summed[2],
        summed[3],
        summed[4],
        summed[5],
        summed[6],
        summed[7],
        summed[8],
        summed[9],
        summed[10],
        summed[11],
        summed[12],
        summed[13],
        summed[14],
        head_peak,
        weight_query * column_factor[None, :],
        weight_key * column_factor[None, :],
    )


def solution(mesh):
    in_specs = (
        P(("dp", "row", "col"), None),
        P(("dp", "row", "col")),
        P(("dp", "row", "col"), None),
        P("row", "col"),
        P("row", "col"),
        P("row", "col"),
        P("row", "col"),
        P("row", "col"),
        P("row", "col"),
        P(("row", "col")),
        P(("row", "col")),
        P(("row", "col")),
        P(("row", "col")),
        P(("row", "col")),
        P(("row", "col")),
        P(("row", "col")),
        P(("row", "col")),
        P(("row", "col")),
        P(),
        P(),
    )
    out_specs = (
        P(("dp", "row", "col"), None),
        P(("dp", "row", "col"), None),
        P("row", "col"),
        P("row", "col"),
        P("row", "col"),
        P("row", "col"),
        P("row", "col"),
        P("row", "col"),
        P(("row", "col")),
        P(("row", "col")),
        P(("row", "col")),
        P(("row", "col")),
        P(("row", "col")),
        P(("row", "col")),
        P(("row", "col")),
        P(("row", "col")),
        P(("row", "col")),
        P(),
        P("row", "col"),
        P("row", "col"),
    )
    return jax.shard_map(
        on_device, mesh=mesh, in_specs=in_specs, out_specs=out_specs, check_vma=False
    )
```

profile of v0, /device:TPU:0, one launch (start us, length us, event | category | flops | bytes accessed | tf_op | source)
XLA Modules:
  0.0 1225.3 jit_solution(10910382905271209997)
XLA Ops:
  7.2 1.9 convert_element_type.496
  9.2 1.8 convert_element_type.501
  11.1 1.8 convert_element_type.491
  12.9 1.8 convert_element_type.508
  16.0 2.8 convert_element_type.519
  19.2 22.3 %all-gather.16 = bf16[8,1,128]{2,1,0:T(2,128)(2,1)S(1)} all-gather(bf16[1,1,128]{2,1,0:T(2,128)(2,1)S(1)} %convert_bitcast_fusion.16), channel_id=5, replica_groups=mesh['dp'=4,'row'=2,'col'=4] {'row','col'}, dimensions={0}, use_global_device_ids=true | all-gather | bytes 2304 | tf_op jit(solution)/shard_map/all_gather | solution.py:92
  41.5 16.7 %all-gather.15 = bf16[8,1,128]{2,1,0:T(2,128)(2,1)S(1)} all-gather(bf16[1,1,128]{2,1,0:T(2,128)(2,1)S(1)} %convert_bitcast_fusion.17), channel_id=3, replica_groups=mesh['dp'=4,'row'=2,'col'=4] {'row','col'}, dimensions={0}, use_global_device_ids=true | all-gather | bytes 2304 | tf_op jit(solution)/shard_map/all_gather | solution.py:93
  58.2 18.9 %all-gather.17 = bf16[8,1,128]{2,1,0:T(2,128)(2,1)S(1)} all-gather(bf16[1,1,128]{2,1,0:T(2,128)(2,1)S(1)} %convert_bitcast_fusion.15), channel_id=8, replica_groups=mesh['dp'=4,'row'=2,'col'=4] {'row','col'}, dimensions={0}, use_global_device_ids=true | all-gather | bytes 2304 | tf_op jit(solution)/shard_map/all_gather | solution.py:94
  77.1 16.3 %all-gather.18 = bf16[8,1,128]{2,1,0:T(2,128)(2,1)S(1)} all-gather(bf16[1,1,128]{2,1,0:T(2,128)(2,1)S(1)} %convert_bitcast_fusion.14), channel_id=9, replica_groups=mesh['dp'=4,'row'=2,'col'=4] {'row','col'}, dimensions={0}, use_global_device_ids=true | all-gather | bytes 2304 | tf_op jit(solution)/shard_map/all_gather | solution.py:97
  93.4 18.8 %all-gather.19 = bf16[8,1,128]{2,1,0:T(2,128)(2,1)S(1)} all-gather(bf16[1,1,128]{2,1,0:T(2,128)(2,1)S(1)} %convert_bitcast_fusion.13), channel_id=10, replica_groups=mesh['dp'=4,'row'=2,'col'=4] {'row','col'}, dimensions={0}, use_global_device_ids=true | all-gather | bytes 2304 | tf_op jit(solution)/shard_map/all_gather | solution.py:98
  112.3 27.1 %all-gather.20 = bf16[8,1,512]{2,1,0:T(2,128)(2,1)S(1)} all-gather(bf16[1,1,512]{2,1,0:T(2,128)(2,1)S(1)} %reshape.565), channel_id=12, replica_groups=mesh['dp'=4,'row'=2,'col'=4] {'row','col'}, dimensions={0}, use_global_device_ids=true | all-gather | bytes 9216 | tf_op jit(solution)/shard_map/all_gather | solution.py:95
  139.4 16.5 %all-gather.21 = bf16[8,1,128]{2,1,0:T(2,128)(2,1)S(1)} all-gather(bf16[1,1,128]{2,1,0:T(2,128)(2,1)S(1)} %convert_bitcast_fusion.12), channel_id=14, replica_groups=mesh['dp'=4,'row'=2,'col'=4] {'row','col'}, dimensions={0}, use_global_device_ids=true | all-gather | bytes 2304 | tf_op jit(solution)/shard_map/all_gather | solution.py:96
  156.5 18.5 %all-gather.22 = bf16[8,1,128]{2,1,0:T(2,128)(2,1)S(1)} all-gather(bf16[1,1,128]{2,1,0:T(2,128)(2,1)S(1)} %convert_bitcast_fusion.11), channel_id=15, replica_groups=mesh['dp'=4,'row'=2,'col'=4] {'row','col'}, dimensions={0}, use_global_device_ids=true | all-gather | bytes 2304 | tf_op jit(solution)/shard_map/all_gather | solution.py:99
  175.6 16.3 %all-gather.23 = bf16[8,1,128]{2,1,0:T(2,128)(2,1)S(1)} all-gather(bf16[1,1,128]{2,1,0:T(2,128)(2,1)S(1)} %convert_bitcast_fusion.10), channel_id=16, replica_groups=mesh['dp'=4,'row'=2,'col'=4] {'row','col'}, dimensions={0}, use_global_device_ids=true | all-gather | bytes 2304 | tf_op jit(solution)/shard_map/all_gather | solution.py:100
  192.8 2.8 copy.182
  195.6 2.3 fusion.30
  199.4 4.5 copy.185
  203.9 3.8 bitcast_convert_fusion.1
  209.2 4.5 copy.179
  213.7 3.8 fusion.31
  219.1 4.5 copy.189
  223.7 7.4 fusion.77
  231.1 8.4 fusion
  239.5 8.3 fusion.37
  250.0 89.6 %all-gather.41.cloned.1.call-done = bf16[16384,256]{1,0:T(8,128)(2,1)} async-done(((bf16[2048,256]{1,0:T(8,128)(2,1)}), bf16[16384,256]{1,0:T(8,128)(2,1)}) %all-gather.41.cloned.1.call-update) | async-done | bytes 8388624 | tf_op jit(solution)/shard_map/all_gather | solution.py:91
  339.6 11.7 copy.193
  351.3 7.2 copy.195
  358.5 106.4 %all-gather.39.cloned.1.call-done = bf16[4096,1024]{1,0:T(8,128)(2,1)} async-done(((bf16[512,1024]{1,0:T(8,128)(2,1)}), bf16[4096,1024]{1,0:T(8,128)(2,1)}) %all-gather.39.cloned.1.call-update) | async-done | bytes 8388624 | tf_op jit(solution)/shard_map/all_gather | solution.py:90
  464.9 11.4 copy.191
  476.3 7.6 copy.197
  483.9 25.6 %multiply_convert_fusion.1 = (bf16[512,4096]{1,0:T(8,128)(2,1)S(1)}, f32[512,4096]{1,0:T(8,128)}, f32[512,4096,1]{1,0,2:T(8,128)}) fusion(f32[4096]{0:T(1024)S(1)} %bitcast.410, bf16[4096,512,2]{1,0,2:T(8,128)(2,1)} %bitcast.352, bf16[64,2,8,512]{3,2,1,0:T(8,128)(2,1)S(1)} %bitcast.393), kind=kOutput, calls=%fused_computation.24 | convolution fusion | flops 4433379328 | bytes 30425088 | tf_op jit(solution)/shard_map/trk,rckn->tcn/dot_general | solution.py:26
  509.5 9.4 fusion.79
  520.7 2.1 fusion.75
  525.0 14.8 %fusion.80 = (bf16[4096]{0:T(1024)(128)(2,1)}, bf16[512,4096]{1,0:T(8,128)(2,1)}) fusion(f32[512,4096]{1,0:T(8,128)} %get-tuple-element.61, bf16[4096,4,256]{2,0,1:T(8,128)(2,1)} %bitcast.350, bf16[64,4,8,256]{3,2,1,0:T(8,128)(2,1)S(1)} %bitcast.370, f32[4096]{0:T(1024)S(1)} %bitcast.411, f32[512,4096,1]{1,0,2:T(8,128)} %get-tuple-element.69), kind=kOutput, calls=%fused_computation.166 | convolution fusion | flops 4328517632 | bytes 30433280 | tf_op jit(solution)/shard_map/tcn,rckn->trk/dot_general | solution.py:38
  539.8 8.5 multiply_reduce_fusion.2
  552.0 2.6 convert_bitcast_fusion.2
  554.6 4.5 copy.219
  561.8 8.9 bitcast_reduce_fusion
  572.9 2.4 copy.216
  575.4 9.2 fusion.71
  584.5 8.2 multiply_convert_fusion
  594.3 1.8 copy-done
  596.0 2.6 convert_bitcast_fusion.5
  598.6 4.2 copy.212
  603.3 6.0 multiply_convert_fusion.2
  610.4 2.6 convert_bitcast_fusion.4
  613.0 4.2 copy.214
  618.1 9.0 convert_bitcast_fusion
  627.0 11.6 copy.225
  638.8 8.0 reshape.504
  646.8 11.7 convert_bitcast_fusion.1
  658.4 11.6 copy.222
  676.2 38.7 %pmax.7 = f32[16]{0:T(128)S(1)} all-reduce(f32[16]{0:T(128)S(1)} %copy-done.50), channel_id=1, replica_groups=mesh['dp'=4,'row'=2,'col'=4] {'dp','row','col'}, use_global_device_ids=true, to_apply=%region_51.52 | all-reduce | flops 16 | bytes 128 | tf_op jit(solution)/shard_map/pmax | solution.py:209
  715.2 37.1 %all-reduce.9 = (bf16[8,128]{1,0:T(8,128)(2,1)S(1)}, bf16[8,128]{1,0:T(8,128)(2,1)S(1)}, bf16[8,128]{1,0:T(8,128)(2,1)S(1)}, bf16[8,512]{1,0:T(8,128)(2,1)S(1)},...) all-reduce(bf16[8,128]{1,0:T(8,128)(2,1)S(1)} %convert_element_type, ...), channel_id=23, replica_groups=mesh['dp'=4,'row'=2,'col'=4] {'row','col'}, use_global_device_ids=true, to_apply=%region_24.25.clone | all-reduce | flops 12288 | bytes 49152
  755.6 5.9 all-reduce.10
  768.1 70.8 %reduce-scatter.9.cloned.1.call-done = bf16[1,512,256]{2,1,0:T(8,128)(2,1)} async-done(((bf16[8,512,256]{2,1,0:T(8,128)(2,1)}), bf16[1,512,256]{2,1,0:T(8,128)(2,1)}) %reduce-scatter.9.cloned.1.call-update) | async-done | bytes 262160 | tf_op jit(solution)/shard_map/reduce_scatter | solution.py:274
  838.9 150.2 %reduce-scatter.17.cloned.1.call-done = bf16[1,2048,256]{2,1,0:T(8,128)(2,1)} async-done(((bf16[8,2048,256]{2,1,0:T(8,128)(2,1)}), bf16[1,2048,256]{2,1,0:T(8,128)(2,1)}) %reduce-scatter.17.cloned.1.call-update) | async-done | bytes 1048592 | tf_op jit(solution)/shard_map/reduce_scatter | solution.py:286
  989.1 150.1 %reduce-scatter.15.cloned.1.call-done = bf16[1,512,1024]{2,1,0:T(8,128)(2,1)} async-done(((bf16[8,512,1024]{2,1,0:T(8,128)(2,1)}), bf16[1,512,1024]{2,1,0:T(8,128)(2,1)}) %reduce-scatter.15.cloned.1.call-update) | async-done | bytes 1048592 | tf_op jit(solution)/shard_map/reduce_scatter | solution.py:283
  1139.3 2.2 broadcast_multiply_fusion
  1141.5 3.0 fusion.81
  1146.4 2.9 bitcast_add_fusion.1
  1149.3 60.4 %all-reduce.14.cloned.1.call-done = (bf16[512,256]{1,0:T(8,128)(2,1)}, bf16[512,256]{1,0:T(8,128)(2,1)}, bf16[512,256]{1,0:T(8,128)(2,1)}, bf16[512,256]{1,0:T(8...) async-done(((bf16[512,256]{1,0:T(8,128)(2,1)}, bf16[512,256]{1,0:T(8,128)(2,1)}, bf16[512,256]{1,0:T(8,128)(2,1)}, bf16[512,256]{1,0:T(8,128)(2,1)}, ...) | async-done | bytes 3145744 | tf_op jit(solution)/shard_map/psum | solution.py:318
  1209.7 2.9 convert_element_type.581
  1212.6 2.7 convert_element_type.587
  (243 shorter events, 46.7 us)
Async XLA Ops:
  7.2 7.6 copy-start.18
  7.2 185.6 %all-gather.33.cloned.1.call-start = ((), (), s32[]{:S(2)}) async-start(), calls=%async_computation.13 | async-start | bytes 2359296 | tf_op jit(solution)/shard_map/all_gather | solution.py:86
  9.2 190.2 %all-gather.35.cloned.1.call-start = ((), (), s32[]{:S(2)}) async-start(), calls=%async_computation.14 | async-start | bytes 2359296 | tf_op jit(solution)/shard_map/all_gather | solution.py:87
  11.0 198.2 %all-gather.31.cloned.1.call-start = ((), (), s32[]{:S(2)}) async-start(), calls=%async_computation.12 | async-start | bytes 2359296 | tf_op jit(solution)/shard_map/all_gather | solution.py:88
  12.9 206.2 %all-gather.37.cloned.1.call-start = ((), (), s32[]{:S(2)}) async-start(), calls=%async_computation.15 | async-start | bytes 2359296 | tf_op jit(solution)/shard_map/all_gather | solution.py:89
  14.7 324.9 %all-gather.41.cloned.1.call-start = ((), (), s32[]{:S(2)}) async-start(), calls=%async_computation.17 | async-start | bytes 9437184 | tf_op jit(solution)/shard_map/all_gather | solution.py:91
  15.9 3.1 copy-start.19
  15.9 3.3 copy-start.51
  15.9 25.6 %copy-start.52 = (f32[128]{0:T(128)S(1)}, f32[128]{0:T(128)}, u32[]{:S(2)}) copy-start(f32[128]{0:T(128)} %param.30) | copy-start | bytes 1540
  15.9 42.3 %copy-start.53 = (f32[128]{0:T(128)S(1)}, f32[128]{0:T(128)}, u32[]{:S(2)}) copy-start(f32[128]{0:T(128)} %param.31) | copy-start | bytes 1540
  15.9 61.2 %copy-start.54 = (f32[128]{0:T(128)S(1)}, f32[128]{0:T(128)}, u32[]{:S(2)}) copy-start(f32[128]{0:T(128)} %param.34) | copy-start | bytes 1540
  15.9 77.5 %copy-start.55 = (f32[128]{0:T(128)S(1)}, f32[128]{0:T(128)}, u32[]{:S(2)}) copy-start(f32[128]{0:T(128)} %param.35) | copy-start | bytes 1540
  15.9 96.4 %copy-start.49 = (f32[512]{0:T(512)S(1)}, f32[512]{0:T(512)}, u32[]{:S(2)}) copy-start(f32[512]{0:T(512)} %param.32) | copy-start | bytes 6148
  15.9 123.4 %copy-start.56 = (f32[128]{0:T(128)S(1)}, f32[128]{0:T(128)}, u32[]{:S(2)}) copy-start(f32[128]{0:T(128)} %param.33) | copy-start | bytes 1540
  15.9 140.6 %copy-start.57 = (f32[128]{0:T(128)S(1)}, f32[128]{0:T(128)}, u32[]{:S(2)}) copy-start(f32[128]{0:T(128)} %param.36) | copy-start | bytes 1540
  15.9 159.7 %copy-start.58 = (f32[128]{0:T(128)S(1)}, f32[128]{0:T(128)}, u32[]{:S(2)}) copy-start(f32[128]{0:T(128)} %param.37) | copy-start | bytes 1540
  15.9 176.6 %copy-start.41 = (s32[512]{0:T(512)S(1)}, s32[512]{0:T(512)}, u32[]{:S(2)}) copy-start(s32[512]{0:T(512)} %param.21) | copy-start | bytes 6148
  16.0 448.9 %all-gather.39.cloned.1.call-start = ((), (), s32[]{:S(2)}) async-start(), calls=%async_computation.16 | async-start | bytes 9437184 | tf_op jit(solution)/shard_map/all_gather | solution.py:90
  18.9 747.4 %reduce-scatter.13.cloned.1.call-start = ((), (), s32[]{:S(2)}) async-start(), calls=%async_computation.9 | async-start | bytes 2359296 | tf_op jit(solution)/shard_map/reduce_scatter | solution.py:280
  19.1 194.6 %copy-start.23 = (bf16[512,1024]{1,0:T(8,128)(2,1)}, bf16[512,1024]{1,0:T(8,128)(2,1)S(1)}, u32[]{:S(2)}) copy-start(bf16[512,1024]{1,0:T(8,128)(2,1)S(1)} %convert_element_type.490) | copy-start | bytes 3145732
  199.3 24.3 %copy-start.5 = (bf16[512,1024]{0,1:T(8,128)(2,1)}, bf16[512,1024]{0,1:T(8,128)(2,1)S(1)}, u32[]{:S(2)}) copy-start(bf16[512,1024]{0,1:T(8,128)(2,1)S(1)} %copy.184) | copy-start | bytes 3145732
  209.2 14.5 %copy-start.3 = (bf16[512,1024]{0,1:T(8,128)(2,1)}, bf16[512,1024]{0,1:T(8,128)(2,1)S(1)}, u32[]{:S(2)}) copy-start(bf16[512,1024]{0,1:T(8,128)(2,1)S(1)} %copy.187) | copy-start | bytes 3145732
  219.1 20.4 %copy-start.13 = (bf16[512,1024]{0,1:T(8,128)(2,1)}, bf16[512,1024]{0,1:T(8,128)(2,1)S(1)}, u32[]{:S(2)}) copy-start(bf16[512,1024]{0,1:T(8,128)(2,1)S(1)} %copy.181) | copy-start | bytes 3145732
  231.1 8.4 copy-start.31
  239.5 8.3 copy-start.37
  239.5 8.3 copy-start.20
  239.5 8.3 copy-start.22
  250.0 233.8 %copy-start.28 = (bf16[512,1024]{1,0:T(8,128)(2,1)}, bf16[512,1024]{1,0:T(8,128)(2,1)S(1)}, u32[]{:S(2)}) copy-start(bf16[512,1024]{1,0:T(8,128)(2,1)S(1)} %fusion.32) | copy-start | bytes 3145732
  483.9 25.6 %copy-start.46 = (f32[8,1,128]{2,1,0:T(1,128)S(1)}, f32[8,1,128]{2,1,0:T(1,128)}, u32[]{:S(2)}) copy-start(f32[8,1,128]{2,1,0:T(1,128)} %convert_element_type.645) | copy-start | bytes 12292
  509.5 9.4 copy-start.59
  509.5 9.8 copy-start.11
  509.5 9.8 copy-start.39
  520.7 19.1 %slice-start = ((s8[8388608]{0:T(1024)(128)(4,1)}), s8[4194304]{0:T(1024)(128)(4,1)S(1)}, s32[]{:S(2)}) async-start(s8[8388608]{0:T(1024)(128)(4,1)} %bitcast.347), calls=%async_computation.19 | async-start | bytes 8388608
  525.0 14.8 %copy-start.14 = (bf16[512,1024]{1,0:T(8,128)(2,1)}, bf16[512,1024]{1,0:T(8,128)(2,1)S(1)}, u32[]{:S(2)}) copy-start(bf16[512,1024]{1,0:T(8,128)(2,1)S(1)} %get-tuple-element.53) | copy-start | bytes 3145732
  525.0 14.8 %slice-start.1 = ((s8[8388608]{0:T(1024)(128)(4,1)}), s8[4194304]{0:T(1024)(128)(4,1)S(1)}, s32[]{:S(2)}) async-start(s8[8388608]{0:T(1024)(128)(4,1)} %bitcast.347), calls=%async_computation.20 | async-start | bytes 8388608
  549.1 3.0 copy-start.61
  554.6 4.6 copy-start.10
  559.1 207.2 %reduce-scatter.11.cloned.1.call-start = ((), (), s32[]{:S(2)}) async-start(), calls=%async_computation.8 | async-start | bytes 2359296 | tf_op jit(solution)/shard_map/reduce_scatter | solution.py:277
  561.8 9.9 copy-start.24
  575.3 192.7 %reduce-scatter.7.cloned.1.call-start = ((), (), s32[]{:S(2)}) async-start(), calls=%async_computation.6 | async-start | bytes 2359296 | tf_op jit(solution)/shard_map/reduce_scatter | solution.py:271
  584.5 8.2 copy-start.4
  592.8 3.3 copy-start
  592.8 3.3 copy-start.25
  598.6 4.7 copy-start.6
  602.9 236.0 %reduce-scatter.9.cloned.1.call-start = ((), (), s32[]{:S(2)}) async-start(), calls=%async_computation.7 | async-start | bytes 2359296 | tf_op jit(solution)/shard_map/reduce_scatter | solution.py:274
  613.0 4.3 copy-start.15
  617.2 371.9 %reduce-scatter.17.cloned.1.call-start = ((), (), s32[]{:S(2)}) async-start(), calls=%async_computation.11 | async-start | bytes 9437184 | tf_op jit(solution)/shard_map/reduce_scatter | solution.py:286
  638.7 8.1 copy-start.29
  638.7 500.5 %reduce-scatter.15.cloned.1.call-start = ((), (), s32[]{:S(2)}) async-start(), calls=%async_computation.10 | async-start | bytes 9437184 | tf_op jit(solution)/shard_map/reduce_scatter | solution.py:283
  670.1 539.6 %all-reduce.14.cloned.1.call-start = ((), (), s32[]{:S(2)}) async-start(), calls=%async_computation.18 | async-start | bytes 6291456 | tf_op jit(solution)/shard_map/psum | solution.py:318
  672.3 3.8 copy-start.9
  674.6 40.5 %copy-start.45 = (bf16[4096]{0:T(1024)(128)(2,1)S(1)}, bf16[4096]{0:T(1024)(128)(2,1)}, u32[]{:S(2)}) copy-start(bf16[4096]{0:T(1024)(128)(2,1)} %get-tuple-element.78) | copy-start | bytes 24580
  674.6 40.6 %copy-start.42 = (bf16[1024]{0:T(1024)(128)(2,1)S(1)}, bf16[1024]{0:T(1024)(128)(2,1)}, u32[]{:S(2)}) copy-start(bf16[1024]{0:T(1024)(128)(2,1)} %get-tuple-element.26) | copy-start | bytes 6148
  674.6 40.6 %copy-start.43 = (bf16[1024]{0:T(1024)(128)(2,1)S(1)}, bf16[1024]{0:T(1024)(128)(2,1)}, u32[]{:S(2)}) copy-start(bf16[1024]{0:T(1024)(128)(2,1)} %get-tuple-element.52) | copy-start | bytes 6148
  674.6 40.6 %copy-start.44 = (bf16[1024]{0:T(1024)(128)(2,1)S(1)}, bf16[1024]{0:T(1024)(128)(2,1)}, u32[]{:S(2)}) copy-start(bf16[1024]{0:T(1024)(128)(2,1)} %get-tuple-element.54) | copy-start | bytes 6148
  674.6 40.6 %copy-start.47 = (bf16[1024]{0:T(1024)(128)(2,1)S(1)}, bf16[1024]{0:T(1024)(128)(2,1)}, u32[]{:S(2)}) copy-start(bf16[1024]{0:T(1024)(128)(2,1)} %get-tuple-element.24) | copy-start | bytes 6148
  674.6 40.6 %copy-start.48 = (bf16[1024]{0:T(1024)(128)(2,1)S(1)}, bf16[1024]{0:T(1024)(128)(2,1)}, u32[]{:S(2)}) copy-start(bf16[1024]{0:T(1024)(128)(2,1)} %get-tuple-element.27) | copy-start | bytes 6148
  714.9 429.6 %copy-start.63 = (f32[16]{0:T(128)}, f32[16]{0:T(128)S(1)}, u32[]{:S(2)}) copy-start(f32[16]{0:T(128)S(1)} %pmax.7) | copy-start | bytes 196
  1141.5 3.1 copy-start.21
  1141.5 3.1 copy-start.27
  1209.7 5.6 copy-start.36
  1209.7 6.4 copy-start.35
  1209.7 7.2 copy-start.34
  1209.7 8.1 copy-start.33
  (15 other events, 22.4 us)
Sparse Core Ops, SparseCore 0:
  10.7 51.8 all-gather.32
  65.3 47.7 all-gather.34
  115.8 47.7 all-gather.30
  166.1 47.9 all-gather.36
  216.6 122.9 all-gather.40
  342.2 122.6 all-gather.38
  559.3 66.4 reduce-scatter.12
  629.3 67.8 reduce-scatter.10
  700.7 67.3 reduce-scatter.6
  771.4 67.4 reduce-scatter.8
  842.5 146.5 reduce-scatter.16
  992.6 146.5 reduce-scatter.14
  1142.0 67.6 all-reduce.13
where the time goes:
time: 1240 us; the launch traced here: 1230 us
  waiting for transfers between devices  630 us (51%)
  blocking collectives  253 us (20%)
  matrix products  149 us (12%)
  local copies, waits for them, and re-layouts  123 us (10%)
  other arithmetic  52.9 us (4%)
  between operations  16.5 us (1%)
    reduce_scatter x1, waiting for transfers between devices, on_device(): lax.psum_scatter(terms[5].astype(jnp.bfloat16), ('row', 'col'), scatter_d...  150 us
    reduce_scatter x1, waiting for transfers between devices, on_device(): lax.psum_scatter(terms[4].astype(jnp.bfloat16), ('row', 'col'), scatter_d...  150 us
    all_gather x1, waiting for transfers between devices, fetch_params(): lax.all_gather(wire_items[4], ('row', 'col'), axis=0, tiled=True)  106 us
    all_gather x1, waiting for transfers between devices, fetch_params(): lax.all_gather(wire_items[5], ('row', 'col'), axis=0, tiled=True)  89.6 us
    reduce_scatter x1, waiting for transfers between devices, on_device(): lax.psum_scatter(terms[1].astype(jnp.bfloat16), ('row', 'col'), scatter_d...  70.8 us
    psum x1, waiting for transfers between devices, on_device(): lax.psum(parted[0][0].astype(jnp.bfloat16), 'dp').astype(jnp.float32)  60.4 us
    reshape x12, local copies, waits for them, and re-layouts, unpack(): shard_item.reshape(row_count, col_count, shard_item.shape[1], shard_item....  57.4 us
    dot_general x6, matrix products, apply_weight(): jnp.einsum('trk,rckn->tcn', operand.reshape(token_count, row_count, rows_...  46.4 us
  transfers between devices with their start and end apart: 13, of which 7 were waited for; matrix products, arithmetic and copies ran while one was open for 17% of the time, Pallas kernels for 0%

commit v1 on v0

--- a/solution.py
+++ b/solution.py
@@ -8,6 +8,12 @@
 SEQ = 512
 norm_eps = 1e-12
 neg_fill = -1e30
+
+
+def add_all(x, name):
+    pieces = lax.all_gather(x, name, axis=0, tiled=False)
+    summed = pieces.sum(axis=0)
+    return summed
 
 
 def norm_rows(values, gain_vec, shift_vec):
@@ -315,7 +321,7 @@
         ).astype(jnp.float32),
     )
     summed = (
-        lax.psum(parted[0][0].astype(jnp.bfloat16), "dp").astype(jnp.float32),
+        add_all(parted[0][0].astype(jnp.bfloat16), "dp").astype(jnp.float32),
         lax.psum(parted[1][0].astype(jnp.bfloat16), "dp").astype(jnp.float32),
         lax.psum(parted[2][0].astype(jnp.bfloat16), "dp").astype(jnp.float32),
         lax.psum(parted[3][0].astype(jnp.bfloat16), "dp").astype(jnp.float32),

time: 1240 us -> 1280 us (1.032)
  waiting for transfers between devices: 630 us -> 665 us
    reduce_scatter x1, waiting for transfers between devices: 0.02 us -> 36.6 us  [on_device(): lax.psum_scatter(terms[2].astype(jnp.bfloat16), ('row', 'col'), scatter_d...]
  transfers between devices with their start and end apart: 13 -> 14, of which waited for: 7 -> 7; matrix products, arithmetic and copies ran while one was open for 17% -> 15% of each run, Pallas kernels for 0% -> 0%
where the time goes in v1:
time: 1280 us; the launch traced here: 1270 us
  waiting for transfers between devices  665 us (52%)
  blocking collectives  254 us (20%)
  matrix products  154 us (12%)
  local copies, waits for them, and re-layouts  124 us (10%)
  other arithmetic  54.8 us (4%)
  between operations  16.7 us (1%)
    reduce_scatter x1, waiting for transfers between devices, on_device(): lax.psum_scatter(terms[5].astype(jnp.bfloat16), ('row', 'col'), scatter_d...  150 us
    reduce_scatter x1, waiting for transfers between devices, on_device(): lax.psum_scatter(terms[4].astype(jnp.bfloat16), ('row', 'col'), scatter_d...  150 us
    all_gather x1, waiting for transfers between devices, fetch_params(): lax.all_gather(wire_items[4], ('row', 'col'), axis=0, tiled=True)  106 us
    all_gather x1, waiting for transfers between devices, fetch_params(): lax.all_gather(wire_items[5], ('row', 'col'), axis=0, tiled=True)  87.7 us
    reduce_scatter x1, waiting for transfers between devices, on_device(): lax.psum_scatter(terms[1].astype(jnp.bfloat16), ('row', 'col'), scatter_d...  71.4 us
    psum x1, waiting for transfers between devices, on_device(): lax.psum(parted[1][0].astype(jnp.bfloat16), 'dp').astype(jnp.float32)  62.1 us
    reshape x12, local copies, waits for them, and re-layouts, unpack(): shard_item.reshape(row_count, col_count, shard_item.shape[1], shard_item....  58.6 us
    dot_general x6, matrix products, apply_weight(): jnp.einsum('trk,rckn->tcn', operand.reshape(token_count, row_count, rows_...  46.8 us
  transfers between devices with their start and end apart: 14, of which 7 were waited for; matrix products, arithmetic and copies ran while one was open for 15% of the time, Pallas kernels for 0%

profile of v1, /device:TPU:0, one launch (start us, length us, event | category | flops | bytes accessed | tf_op | source)
XLA Modules:
  0.0 1269.4 jit_solution(3396390480290758911)
XLA Ops:
  7.2 1.9 convert_element_type.508
  9.2 1.8 convert_element_type.496
  11.1 1.8 convert_element_type.501
  12.9 1.8 convert_element_type.491
  16.0 2.9 convert_element_type.519
  19.2 22.3 %all-gather.16 = bf16[8,1,128]{2,1,0:T(2,128)(2,1)S(1)} all-gather(bf16[1,1,128]{2,1,0:T(2,128)(2,1)S(1)} %convert_bitcast_fusion.16), channel_id=5, replica_groups=mesh['dp'=4,'row'=2,'col'=4] {'row','col'}, dimensions={0}, use_global_device_ids=true | all-gather | bytes 2304 | tf_op jit(solution)/shard_map/all_gather | solution.py:98
  41.5 16.7 %all-gather.15 = bf16[8,1,128]{2,1,0:T(2,128)(2,1)S(1)} all-gather(bf16[1,1,128]{2,1,0:T(2,128)(2,1)S(1)} %convert_bitcast_fusion.17), channel_id=3, replica_groups=mesh['dp'=4,'row'=2,'col'=4] {'row','col'}, dimensions={0}, use_global_device_ids=true | all-gather | bytes 2304 | tf_op jit(solution)/shard_map/all_gather | solution.py:99
  58.3 18.8 %all-gather.17 = bf16[8,1,128]{2,1,0:T(2,128)(2,1)S(1)} all-gather(bf16[1,1,128]{2,1,0:T(2,128)(2,1)S(1)} %convert_bitcast_fusion.15), channel_id=8, replica_groups=mesh['dp'=4,'row'=2,'col'=4] {'row','col'}, dimensions={0}, use_global_device_ids=true | all-gather | bytes 2304 | tf_op jit(solution)/shard_map/all_gather | solution.py:100
  77.1 16.3 %all-gather.18 = bf16[8,1,128]{2,1,0:T(2,128)(2,1)S(1)} all-gather(bf16[1,1,128]{2,1,0:T(2,128)(2,1)S(1)} %convert_bitcast_fusion.14), channel_id=9, replica_groups=mesh['dp'=4,'row'=2,'col'=4] {'row','col'}, dimensions={0}, use_global_device_ids=true | all-gather | bytes 2304 | tf_op jit(solution)/shard_map/all_gather | solution.py:103
  93.4 18.8 %all-gather.19 = bf16[8,1,128]{2,1,0:T(2,128)(2,1)S(1)} all-gather(bf16[1,1,128]{2,1,0:T(2,128)(2,1)S(1)} %convert_bitcast_fusion.13), channel_id=10, replica_groups=mesh['dp'=4,'row'=2,'col'=4] {'row','col'}, dimensions={0}, use_global_device_ids=true | all-gather | bytes 2304 | tf_op jit(solution)/shard_map/all_gather | solution.py:104
  112.3 27.1 %all-gather.20 = bf16[8,1,512]{2,1,0:T(2,128)(2,1)S(1)} all-gather(bf16[1,1,512]{2,1,0:T(2,128)(2,1)S(1)} %reshape.564), channel_id=12, replica_groups=mesh['dp'=4,'row'=2,'col'=4] {'row','col'}, dimensions={0}, use_global_device_ids=true | all-gather | bytes 9216 | tf_op jit(solution)/shard_map/all_gather | solution.py:101
  139.4 16.5 %all-gather.21 = bf16[8,1,128]{2,1,0:T(2,128)(2,1)S(1)} all-gather(bf16[1,1,128]{2,1,0:T(2,128)(2,1)S(1)} %convert_bitcast_fusion.12), channel_id=14, replica_groups=mesh['dp'=4,'row'=2,'col'=4] {'row','col'}, dimensions={0}, use_global_device_ids=true | all-gather | bytes 2304 | tf_op jit(solution)/shard_map/all_gather | solution.py:102
  156.5 18.5 %all-gather.22 = bf16[8,1,128]{2,1,0:T(2,128)(2,1)S(1)} all-gather(bf16[1,1,128]{2,1,0:T(2,128)(2,1)S(1)} %convert_bitcast_fusion.11), channel_id=15, replica_groups=mesh['dp'=4,'row'=2,'col'=4] {'row','col'}, dimensions={0}, use_global_device_ids=true | all-gather | bytes 2304 | tf_op jit(solution)/shard_map/all_gather | solution.py:105
  175.6 16.3 %all-gather.23 = bf16[8,1,128]{2,1,0:T(2,128)(2,1)S(1)} all-gather(bf16[1,1,128]{2,1,0:T(2,128)(2,1)S(1)} %convert_bitcast_fusion.10), channel_id=16, replica_groups=mesh['dp'=4,'row'=2,'col'=4] {'row','col'}, dimensions={0}, use_global_device_ids=true | all-gather | bytes 2304 | tf_op jit(solution)/shard_map/all_gather | solution.py:106
  192.8 4.3 copy.189
  198.5 2.8 copy.182
  201.3 2.3 fusion.30
  205.1 4.5 copy.185
  209.6 3.9 bitcast_convert_fusion.1
  215.0 4.5 copy.179
  219.5 3.9 fusion.31
  225.0 7.5 fusion.77
  232.4 8.3 fusion
  240.8 8.0 fusion.37
  251.7 87.7 %all-gather.44.cloned.1.call-done = bf16[16384,256]{1,0:T(8,128)(2,1)} async-done(((bf16[2048,256]{1,0:T(8,128)(2,1)}), bf16[16384,256]{1,0:T(8,128)(2,1)}) %all-gather.44.cloned.1.call-update) | async-done | bytes 8388624 | tf_op jit(solution)/shard_map/all_gather | solution.py:97
  339.4 11.7 copy.193
  351.1 7.2 copy.195
  358.3 105.7 %all-gather.42.cloned.1.call-done = bf16[4096,1024]{1,0:T(8,128)(2,1)} async-done(((bf16[512,1024]{1,0:T(8,128)(2,1)}), bf16[4096,1024]{1,0:T(8,128)(2,1)}) %all-gather.42.cloned.1.call-update) | async-done | bytes 8388624 | tf_op jit(solution)/shard_map/all_gather | solution.py:96
  464.0 11.5 copy.191
  475.5 7.6 copy.197
  483.1 25.7 %multiply_convert_fusion.1 = (bf16[512,4096]{1,0:T(8,128)(2,1)S(1)}, f32[512,4096]{1,0:T(8,128)}, f32[512,4096,1]{1,0,2:T(8,128)}) fusion(f32[4096]{0:T(1024)S(1)} %bitcast.410, bf16[4096,512,2]{1,0,2:T(8,128)(2,1)} %bitcast.353, bf16[64,2,8,512]{3,2,1,0:T(8,128)(2,1)S(1)} %bitcast.392), kind=kOutput, calls=%fused_computation.24 | convolution fusion | flops 4433379328 | bytes 30425088 | tf_op jit(solution)/shard_map/trk,rckn->tcn/dot_general | solution.py:32
  508.9 9.6 fusion.79
  520.3 2.1 fusion.75
  524.6 14.8 %fusion.80 = (bf16[4096]{0:T(1024)(128)(2,1)}, bf16[512,4096]{1,0:T(8,128)(2,1)}) fusion(f32[512,4096]{1,0:T(8,128)} %get-tuple-element.60, bf16[4096,4,256]{2,0,1:T(8,128)(2,1)} %bitcast.351, bf16[64,4,8,256]{3,2,1,0:T(8,128)(2,1)S(1)} %bitcast.371, f32[4096]{0:T(1024)S(1)} %bitcast.411, f32[512,4096,1]{1,0,2:T(8,128)} %get-tuple-element.68), kind=kOutput, calls=%fused_computation.166 | convolution fusion | flops 4328517632 | bytes 30433280 | tf_op jit(solution)/shard_map/tcn,rckn->trk/dot_general | solution.py:44
  539.4 8.6 multiply_reduce_fusion.2
  553.8 14.9 %fusion.71 = (f32[16]{0:T(128)}, f32[16,512]{1,0:T(8,128)}, f32[16,512,512]{1,2,0:T(8,128)}) fusion(f32[16,512,512]{1,2,0:T(8,128)} %get-tuple-element.65, f32[16,512]{1,0:T(8,128)} %log_add_fusion, bf16[512,16,64]{0,2,1:T(8,128)(2,1)S(1)} %bitcast.346, bf16[512,16,64]{0,2,1:T(8,128)(2,1)} %bitcast.368), kind=kOutput, calls=%fused_computation.158 | convolution fusion | flops 553639936 | bytes 35717184 | tf_op jit(solution)/shard_map/sqhd,skhd->shqk/dot_general | solution.py:236
  570.6 8.0 multiply_convert_fusion
  580.2 1.8 copy-done
  582.9 2.6 convert_bitcast_fusion.5
  585.5 4.2 copy.212
  591.4 2.8 convert_bitcast_fusion.2
  594.2 2.4 copy.219
  596.7 8.7 bitcast_reduce_fusion
  607.7 2.4 copy.216
  610.4 6.1 multiply_convert_fusion.2
  618.8 2.3 copy.214
  622.0 9.0 convert_bitcast_fusion
  631.0 11.5 copy.225
  642.6 8.0 reshape.503
  650.6 11.7 convert_bitcast_fusion.1
  662.3 11.5 copy.222
  680.7 38.5 %pmax.7 = f32[16]{0:T(128)S(1)} all-reduce(f32[16]{0:T(128)S(1)} %copy-done.52), channel_id=1, replica_groups=mesh['dp'=4,'row'=2,'col'=4] {'dp','row','col'}, use_global_device_ids=true, to_apply=%region_51.52 | all-reduce | flops 16 | bytes 128 | tf_op jit(solution)/shard_map/pmax | solution.py:215
  719.5 37.4 %all-reduce.9 = (bf16[8,128]{1,0:T(8,128)(2,1)S(1)}, bf16[8,128]{1,0:T(8,128)(2,1)S(1)}, bf16[8,128]{1,0:T(8,128)(2,1)S(1)}, bf16[8,512]{1,0:T(8,128)(2,1)S(1)},...) all-reduce(bf16[8,128]{1,0:T(8,128)(2,1)S(1)} %convert_element_type, ...), channel_id=23, replica_groups=mesh['dp'=4,'row'=2,'col'=4] {'row','col'}, use_global_device_ids=true, to_apply=%region_24.25.clone | all-reduce | flops 12288 | bytes 49152
  759.7 2.3 broadcast_multiply_fusion
  761.9 36.6 %reduce-scatter.11.cloned.1.call-done = bf16[1,512,256]{2,1,0:T(8,128)(2,1)} async-done(((bf16[8,512,256]{2,1,0:T(8,128)(2,1)}), bf16[1,512,256]{2,1,0:T(8,128)(2,1)}) %reduce-scatter.11.cloned.1.call-update) | async-done | bytes 262160 | tf_op jit(solution)/shard_map/reduce_scatter | solution.py:283
  798.5 71.4 %reduce-scatter.9.cloned.1.call-done = bf16[1,512,256]{2,1,0:T(8,128)(2,1)} async-done(((bf16[8,512,256]{2,1,0:T(8,128)(2,1)}), bf16[1,512,256]{2,1,0:T(8,128)(2,1)}) %reduce-scatter.9.cloned.1.call-update) | async-done | bytes 262160 | tf_op jit(solution)/shard_map/reduce_scatter | solution.py:280
  869.9 150.1 %reduce-scatter.17.cloned.1.call-done = bf16[1,2048,256]{2,1,0:T(8,128)(2,1)} async-done(((bf16[8,2048,256]{2,1,0:T(8,128)(2,1)}), bf16[1,2048,256]{2,1,0:T(8,128)(2,1)}) %reduce-scatter.17.cloned.1.call-update) | async-done | bytes 1048592 | tf_op jit(solution)/shard_map/reduce_scatter | solution.py:292
  1020.1 150.1 %reduce-scatter.15.cloned.1.call-done = bf16[1,512,1024]{2,1,0:T(8,128)(2,1)} async-done(((bf16[8,512,1024]{2,1,0:T(8,128)(2,1)}), bf16[1,512,1024]{2,1,0:T(8,128)(2,1)}) %reduce-scatter.15.cloned.1.call-update) | async-done | bytes 1048592 | tf_op jit(solution)/shard_map/reduce_scatter | solution.py:289
  1170.8 6.6 all-reduce.10
  1182.1 3.0 fusion.81
  1187.1 2.9 bitcast_add_fusion.1
  1192.3 62.1 %all-reduce.14.cloned.1.call-done = (bf16[512,256]{1,0:T(8,128)(2,1)}, bf16[512,256]{1,0:T(8,128)(2,1)}, bf16[512,256]{1,0:T(8,128)(2,1)}, bf16[512,1024]{1,0:T(8,128)(2,1)}, bf16[2048,256]{1,0:T(8,128)(2,1)}) async-done(((bf16[512,256]{1,0:T(8,128)(2,1)}, bf16[512,256]{1,0:T(8,128)(2,1)}, bf16[512,256]{1,0:T(8,128)(2,1)}, bf16[512,1024]{1,0:T(8,128)(2,1)}, bf16[2048,256]{1,0:T(8,128)(2,1)}), ...) | async-done | bytes 2883600 | tf_op jit(solution)/shard_map/psum | solution.py:325
  1254.4 2.9 convert_element_type.580
  1257.2 2.7 convert_element_type.586
  (258 shorter events, 54.3 us)
Async XLA Ops:
  7.2 7.6 copy-start.22
  7.2 185.5 %all-gather.40.cloned.1.call-start = ((), (), s32[]{:S(2)}) async-start(), calls=%async_computation.16 | async-start | bytes 2359296 | tf_op jit(solution)/shard_map/all_gather | solution.py:95
  9.2 189.3 %all-gather.36.cloned.1.call-start = ((), (), s32[]{:S(2)}) async-start(), calls=%async_computation.14 | async-start | bytes 2359296 | tf_op jit(solution)/shard_map/all_gather | solution.py:92
  11.0 194.1 %all-gather.38.cloned.1.call-start = ((), (), s32[]{:S(2)}) async-start(), calls=%async_computation.15 | async-start | bytes 2359296 | tf_op jit(solution)/shard_map/all_gather | solution.py:93
  12.9 202.2 %all-gather.34.cloned.1.call-start = ((), (), s32[]{:S(2)}) async-start(), calls=%async_computation.13 | async-start | bytes 2359296 | tf_op jit(solution)/shard_map/all_gather | solution.py:94
  14.7 324.7 %all-gather.44.cloned.1.call-start = ((), (), s32[]{:S(2)}) async-start(), calls=%async_computation.18 | async-start | bytes 9437184 | tf_op jit(solution)/shard_map/all_gather | solution.py:97
  15.9 3.3 copy-start.53
  15.9 25.7 %copy-start.54 = (f32[128]{0:T(128)S(1)}, f32[128]{0:T(128)}, u32[]{:S(2)}) copy-start(f32[128]{0:T(128)} %param.30) | copy-start | bytes 1540
  15.9 42.4 %copy-start.55 = (f32[128]{0:T(128)S(1)}, f32[128]{0:T(128)}, u32[]{:S(2)}) copy-start(f32[128]{0:T(128)} %param.31) | copy-start | bytes 1540
  15.9 61.2 %copy-start.56 = (f32[128]{0:T(128)S(1)}, f32[128]{0:T(128)}, u32[]{:S(2)}) copy-start(f32[128]{0:T(128)} %param.34) | copy-start | bytes 1540
  15.9 77.5 %copy-start.57 = (f32[128]{0:T(128)S(1)}, f32[128]{0:T(128)}, u32[]{:S(2)}) copy-start(f32[128]{0:T(128)} %param.35) | copy-start | bytes 1540
  15.9 96.3 %copy-start.51 = (f32[512]{0:T(512)S(1)}, f32[512]{0:T(512)}, u32[]{:S(2)}) copy-start(f32[512]{0:T(512)} %param.32) | copy-start | bytes 6148
  15.9 123.4 %copy-start.58 = (f32[128]{0:T(128)S(1)}, f32[128]{0:T(128)}, u32[]{:S(2)}) copy-start(f32[128]{0:T(128)} %param.33) | copy-start | bytes 1540
  15.9 140.6 %copy-start.59 = (f32[128]{0:T(128)S(1)}, f32[128]{0:T(128)}, u32[]{:S(2)}) copy-start(f32[128]{0:T(128)} %param.36) | copy-start | bytes 1540
  15.9 159.7 %copy-start.60 = (f32[128]{0:T(128)S(1)}, f32[128]{0:T(128)}, u32[]{:S(2)}) copy-start(f32[128]{0:T(128)} %param.37) | copy-start | bytes 1540
  15.9 176.6 %copy-start.42 = (s32[512]{0:T(512)S(1)}, s32[512]{0:T(512)}, u32[]{:S(2)}) copy-start(s32[512]{0:T(512)} %param.21) | copy-start | bytes 6148
  16.0 448.0 %all-gather.42.cloned.1.call-start = ((), (), s32[]{:S(2)}) async-start(), calls=%async_computation.17 | async-start | bytes 9437184 | tf_op jit(solution)/shard_map/all_gather | solution.py:96
  18.9 655.0 %reduce-scatter.7.cloned.1.call-start = ((), (), s32[]{:S(2)}) async-start(), calls=%async_computation.6 | async-start | bytes 2359296 | tf_op jit(solution)/shard_map/reduce_scatter | solution.py:277
  19.2 200.4 %copy-start.28 = (bf16[512,1024]{1,0:T(8,128)(2,1)}, bf16[512,1024]{1,0:T(8,128)(2,1)S(1)}, u32[]{:S(2)}) copy-start(bf16[512,1024]{1,0:T(8,128)(2,1)S(1)} %convert_element_type.490) | copy-start | bytes 3145732
  192.7 4.3 copy-start.10
  205.1 19.9 %copy-start.5 = (bf16[512,1024]{0,1:T(8,128)(2,1)}, bf16[512,1024]{0,1:T(8,128)(2,1)S(1)}, u32[]{:S(2)}) copy-start(bf16[512,1024]{0,1:T(8,128)(2,1)S(1)} %copy.184) | copy-start | bytes 3145732
  215.0 10.0 copy-start.3
  225.0 15.8 %copy-start.13 = (bf16[512,1024]{0,1:T(8,128)(2,1)}, bf16[512,1024]{0,1:T(8,128)(2,1)S(1)}, u32[]{:S(2)}) copy-start(bf16[512,1024]{0,1:T(8,128)(2,1)S(1)} %copy.181) | copy-start | bytes 3145732
  240.8 8.0 copy-start.24
  240.8 8.0 copy-start.27
  251.7 231.5 %copy-start.34 = (bf16[512,1024]{1,0:T(8,128)(2,1)}, bf16[512,1024]{1,0:T(8,128)(2,1)S(1)}, u32[]{:S(2)}) copy-start(bf16[512,1024]{1,0:T(8,128)(2,1)S(1)} %fusion.32) | copy-start | bytes 3145732
  483.1 25.7 %copy-start.48 = (f32[8,1,128]{2,1,0:T(1,128)S(1)}, f32[8,1,128]{2,1,0:T(1,128)}, u32[]{:S(2)}) copy-start(f32[8,1,128]{2,1,0:T(1,128)} %convert_element_type.644) | copy-start | bytes 12292
  508.9 9.7 copy-start.61
  508.9 10.1 copy-start.11
  508.9 10.1 copy-start.40
  520.3 19.1 %slice-start.4 = ((s8[8388608]{0:T(1024)(128)(4,1)}), s8[4194304]{0:T(1024)(128)(4,1)S(1)}, s32[]{:S(2)}) async-start(s8[8388608]{0:T(1024)(128)(4,1)} %bitcast.348), calls=%async_computation.24 | async-start | bytes 8388608
  524.6 14.8 %copy-start.14 = (bf16[512,1024]{1,0:T(8,128)(2,1)}, bf16[512,1024]{1,0:T(8,128)(2,1)S(1)}, u32[]{:S(2)}) copy-start(bf16[512,1024]{1,0:T(8,128)(2,1)S(1)} %get-tuple-element.52) | copy-start | bytes 3145732
  524.6 14.8 %slice-start.5 = ((s8[8388608]{0:T(1024)(128)(4,1)}), s8[4194304]{0:T(1024)(128)(4,1)S(1)}, s32[]{:S(2)}) async-start(s8[8388608]{0:T(1024)(128)(4,1)} %bitcast.348), calls=%async_computation.25 | async-start | bytes 8388608
  548.0 3.9 copy-start.26
  553.8 14.9 %slice-start = ((s8[16777216]{0:T(1024)(128)(4,1)}), s8[4194304]{0:T(1024)(128)(4,1)S(1)}, s32[]{:S(2)}) async-start(s8[16777216]{0:T(1024)(128)(4,1)} %bitcast.334), calls=%async_computation.20 | async-start | bytes 8388608
  553.8 14.9 %slice-start.1 = ((s8[16777216]{0:T(1024)(128)(4,1)}), s8[4194304]{0:T(1024)(128)(4,1)S(1)}, s32[]{:S(2)}) async-start(s8[16777216]{0:T(1024)(128)(4,1)} %bitcast.334), calls=%async_computation.21 | async-start | bytes 8388608
  553.8 15.6 %slice-start.2 = ((s8[16777216]{0:T(1024)(128)(4,1)}), s8[4194304]{0:T(1024)(128)(4,1)S(1)}, s32[]{:S(2)}) async-start(s8[16777216]{0:T(1024)(128)(4,1)} %bitcast.334), calls=%async_computation.22 | async-start | bytes 8388608
  553.8 16.8 %slice-start.3 = ((s8[16777216]{0:T(1024)(128)(4,1)}), s8[4194304]{0:T(1024)(128)(4,1)S(1)}, s32[]{:S(2)}) async-start(s8[16777216]{0:T(1024)(128)(4,1)} %bitcast.334), calls=%async_computation.23 | async-start | bytes 8388608
  570.6 8.1 copy-start.4
  578.6 4.3 copy-start.29
  585.5 4.3 copy-start.17
  589.7 172.2 %reduce-scatter.13.cloned.1.call-start = ((), (), s32[]{:S(2)}) async-start(), calls=%async_computation.10 | async-start | bytes 2359296 | tf_op jit(solution)/shard_map/reduce_scatter | solution.py:286
  596.6 9.8 copy-start.30
  596.6 201.9 %reduce-scatter.11.cloned.1.call-start = ((), (), s32[]{:S(2)}) async-start(), calls=%async_computation.9 | async-start | bytes 2359296 | tf_op jit(solution)/shard_map/reduce_scatter | solution.py:283
  610.1 259.8 %reduce-scatter.9.cloned.1.call-start = ((), (), s32[]{:S(2)}) async-start(), calls=%async_computation.8 | async-start | bytes 2359296 | tf_op jit(solution)/shard_map/reduce_scatter | solution.py:280
  610.4 7.1 copy-start.31
  621.1 398.9 %reduce-scatter.17.cloned.1.call-start = ((), (), s32[]{:S(2)}) async-start(), calls=%async_computation.12 | async-start | bytes 9437184 | tf_op jit(solution)/shard_map/reduce_scatter | solution.py:292
  642.5 8.1 copy-start.35
  642.5 527.6 %reduce-scatter.15.cloned.1.call-start = ((), (), s32[]{:S(2)}) async-start(), calls=%async_computation.11 | async-start | bytes 9437184 | tf_op jit(solution)/shard_map/reduce_scatter | solution.py:289
  673.9 516.1 %all-gather.32.cloned.1.call-start = ((), (), s32[]{:S(2)}) async-start(), calls=%async_computation.7 | async-start | bytes 1310720 | tf_op jit(solution)/shard_map/all_gather | solution.py:14
  674.7 579.7 %all-reduce.14.cloned.1.call-start = ((), (), s32[]{:S(2)}) async-start(), calls=%async_computation.19 | async-start | bytes 5767168 | tf_op jit(solution)/shard_map/psum | solution.py:325
  676.7 3.8 copy-start.9
  679.0 40.4 %copy-start.47 = (bf16[4096]{0:T(1024)(128)(2,1)S(1)}, bf16[4096]{0:T(1024)(128)(2,1)}, u32[]{:S(2)}) copy-start(bf16[4096]{0:T(1024)(128)(2,1)} %get-tuple-element.77) | copy-start | bytes 24580
  679.0 40.4 %copy-start.43 = (bf16[1024]{0:T(1024)(128)(2,1)S(1)}, bf16[1024]{0:T(1024)(128)(2,1)}, u32[]{:S(2)}) copy-start(bf16[1024]{0:T(1024)(128)(2,1)} %get-tuple-element.22) | copy-start | bytes 6148
  679.0 40.4 %copy-start.44 = (bf16[1024]{0:T(1024)(128)(2,1)S(1)}, bf16[1024]{0:T(1024)(128)(2,1)}, u32[]{:S(2)}) copy-start(bf16[1024]{0:T(1024)(128)(2,1)} %get-tuple-element.26) | copy-start | bytes 6148
  679.0 40.4 %copy-start.45 = (bf16[1024]{0:T(1024)(128)(2,1)S(1)}, bf16[1024]{0:T(1024)(128)(2,1)}, u32[]{:S(2)}) copy-start(bf16[1024]{0:T(1024)(128)(2,1)} %get-tuple-element.51) | copy-start | bytes 6148
  679.0 40.4 %copy-start.46 = (bf16[1024]{0:T(1024)(128)(2,1)S(1)}, bf16[1024]{0:T(1024)(128)(2,1)}, u32[]{:S(2)}) copy-start(bf16[1024]{0:T(1024)(128)(2,1)} %get-tuple-element.53) | copy-start | bytes 6148
  679.0 40.4 %copy-start.49 = (bf16[1024]{0:T(1024)(128)(2,1)S(1)}, bf16[1024]{0:T(1024)(128)(2,1)}, u32[]{:S(2)}) copy-start(bf16[1024]{0:T(1024)(128)(2,1)} %get-tuple-element.24) | copy-start | bytes 6148
  679.1 40.4 %copy-start.50 = (bf16[1024]{0:T(1024)(128)(2,1)S(1)}, bf16[1024]{0:T(1024)(128)(2,1)}, u32[]{:S(2)}) copy-start(bf16[1024]{0:T(1024)(128)(2,1)} %get-tuple-element.27) | copy-start | bytes 6148
  680.5 501.6 %copy-start.21 = (bf16[16,64,512]{2,1,0:T(8,128)(2,1)S(1)}, bf16[16,64,512]{2,1,0:T(8,128)(2,1)}, u32[]{:S(2)}) copy-start(bf16[16,64,512]{2,1,0:T(8,128)(2,1)} %copy-done.20) | copy-start | bytes 3145732
  719.2 465.9 %copy-start.64 = (f32[16]{0:T(128)}, f32[16]{0:T(128)S(1)}, u32[]{:S(2)}) copy-start(f32[16]{0:T(128)S(1)} %pmax.7) | copy-start | bytes 196
  1254.4 5.6 copy-start.39
  1254.4 6.4 copy-start.38
  1254.4 7.2 copy-start.37
  (21 other events, 42.5 us)
Sparse Core Ops, SparseCore 0:
  10.7 51.8 all-gather.39
  65.3 47.7 all-gather.35
  115.8 47.7 all-gather.37
  166.1 47.6 all-gather.33
  216.3 122.9 all-gather.43
  341.4 122.6 all-gather.41
  589.8 66.4 reduce-scatter.6
  659.9 67.7 reduce-scatter.12
  731.1 67.3 reduce-scatter.10
  802.5 67.3 reduce-scatter.8
  873.5 146.4 reduce-scatter.16
  1023.5 146.5 reduce-scatter.14
  1171.7 15.7 all-gather.31
  1190.1 64.2 all-reduce.13
